TPU v7x, 768 devices: a whole 4x8x12 slice. The times are simulated.
768 devices in a mesh: inter: 24 (over z, y_hi), intra: 32 (over y_lo, x, core).
Axes of the slice: x: 4, y: 8 (y_hi: 2, y_lo: 4; y = y_hi * 4 + y_lo), z: 12, core: 2. Of those that a mesh axis runs over, the one named last changes fastest.
Arguments:
- tokens: bfloat16 [98304, 8192], P(('inter', 'intra'))
- flat_params: bfloat16 [1056768], P(('inter', 'intra'))
- cotangent: bfloat16 [98304, 128], P(('inter', 'intra')), may hold values from -6 to 6
Outputs:
- values: bfloat16 [98304, 128], P(('inter', 'intra'))
- token_grads: bfloat16 [98304, 8192], P(('inter', 'intra'))
- param_grads: float32 [1056768], P(('inter', 'intra'))
All inputs are finite; a program needn't handle non-finite values.
Results may differ from a plain program's by a relative error of at most 0.0049.
Values may be sent and summed in bfloat16 or wider, within the bound.
No kernel may reach another device: no remote copies, remote signals or barrier semaphores. Data moves between devices by JAX's collectives and lax.ppermute only.
A program may use at most 64 MiB of HBM per device.

v0:
```python
import jax
import jax.numpy as jnp
from jax import lax
from jax.sharding import PartitionSpec as P


def on_device(tokens, flat_params, cotangent):
    inter_count = lax.axis_size("inter")
    intra_count = lax.axis_size("intra")
    shard_len = flat_params.shape[0]
    width = tokens.shape[1]
    head_cols = cotangent.shape[1]
    pooled = lax.all_gather(flat_params.reshape(1, shard_len), "inter", axis=0, tiled=True)
    gathered = lax.all_gather(
        pooled.reshape(inter_count, 1, shard_len), "intra", axis=1, tiled=True
    ).reshape(-1)
    gain = gathered[:width].astype(jnp.float32)
    weight = gathered[width:].reshape(width, head_cols)
    as_float = tokens.astype(jnp.float32)
    inverse = lax.rsqrt(jnp.mean(as_float * as_float, axis=1, keepdims=True) + 1e-05)
    normed = as_float * inverse
    hidden = (normed * gain).astype(jnp.bfloat16)
    values = jnp.dot(hidden, weight, preferred_element_type=jnp.float32).astype(jnp.bfloat16)
    weight_grad = lax.dot_general(
        hidden, cotangent, (((0,), (0,)), ((), ())), preferred_element_type=jnp.float32
    )
    back_weight = gathered[width:].reshape(width, head_cols)
    hidden_grad = lax.dot_general(
        cotangent, back_weight, (((1,), (1,)), ((), ())), preferred_element_type=jnp.float32
    )
    gain_grad = jnp.sum(hidden_grad * normed, axis=0)
    normed_grad = hidden_grad * gain
    token_grads = inverse * (
        normed_grad - normed * jnp.mean(normed_grad * normed, axis=1, keepdims=True)
    )
    token_grads = token_grads.astype(jnp.bfloat16)
    partial_grads = jnp.concatenate([gain_grad, weight_grad.reshape(-1)])
    grouped = lax.psum_scatter(
        partial_grads.reshape(inter_count, intra_count, shard_len),
        "intra",
        scatter_dimension=1,
        tiled=True,
    )
    owned = lax.psum_scatter(
        grouped.reshape(inter_count, shard_len), "inter", scatter_dimension=0, tiled=True
    )
    return (values, token_grads, owned.reshape(shard_len))


def solution(mesh):
    in_specs = (P(("inter", "intra"), None), P(("inter", "intra")), P(("inter", "intra"), None))
    out_specs = (P(("inter", "intra"), None), P(("inter", "intra"), None), P(("inter", "intra")))
    return jax.shard_map(
        on_device, mesh=mesh, in_specs=in_specs, out_specs=out_specs, check_vma=False
    )
```

profile of v0, /device:TPU:2, one launch (start us, length us, event | category | flops | bytes accessed | tf_op | source)
XLA Modules:
  0.0 861.0 jit_solution(12014931571521626072)
XLA Ops:
  7.2 0.0 copy-start
  7.2 0.0 all-reduce.6.cloned.1.call-start
  7.2 1.4 fusion.19
  9.3 0.9 dynamic-update-slice
  10.2 0.0 copy-start.2
  10.2 0.6 copy-done.2
  10.8 0.0 all-reduce.6.cloned.1.call-update
  10.8 0.0 all-gather.5.cloned.1.call-start
  10.9 297.4 %all-reduce.6.cloned.1.call-done = bf16[33024]{0:T(1024)(128)(2,1)} async-done(((bf16[33024]{0:T(1024)(128)(2,1)}), bf16[33024]{0:T(1024)(128)(2,1)}) %all-reduce.6.cloned.1.call-update) | async-done | bytes 66064
  308.3 1.7 reshape.51
  309.9 0.0 all-gather.5.cloned.1.call-update
  309.9 0.0 reduce-scatter.5.cloned.1.call-start
  310.0 3.2 copy.16
  313.2 1.1 fusion.10
  314.3 52.5 %all-gather.5.cloned.1.call-done = bf16[32,1376,24]{1,2,0:T(8,128)(2,1)} async-done(((bf16[1,1376,24]{1,2,0:T(8,128)(2,1)}), bf16[32,1376,24]{1,2,0:T(8,128)(2,1)}) %all-gather.5.cloned.1.call-update) | async-done | bytes 2113552 | tf_op jit(solution)/shard_map/all_gather | solution.py:14
  366.9 3.2 copy.17
  370.1 5.6 reshape.59
  375.6 4.2 slice.11
  379.8 1.9 copy.20
  381.7 0.0 copy-start.1
  381.7 0.0 copy-done
  381.7 1.3 convolution_bitcast_fusion
  383.0 0.3 copy-done.1
  383.3 3.9 fusion.9
  387.2 2.1 pad_maximum_fusion
  389.3 6.0 reshape.48
  395.3 6.7 copy.18
  402.0 0.0 reduce-scatter.5.cloned.1.call-update
  402.0 0.0 all-reduce.8.cloned.1.call-start
  402.1 3.9 fusion.8
  406.0 147.9 %reduce-scatter.5.cloned.1.call-done = f32[24,1,1376]{2,0,1:T(8,128)} async-done(((f32[24,32,1376]{2,0,1:T(8,128)}), f32[24,1,1376]{2,0,1:T(8,128)}) %reduce-scatter.5.cloned.1.call-update) | async-done | bytes 132112
  553.9 0.0 all-reduce.8.cloned.1.call-update
  553.9 4.9 fusion.14
  558.8 4.1 copy.19
  562.8 289.7 %all-reduce.8.cloned.1.call-done = f32[24,1376]{1,0:T(8,128)} async-done(((f32[24,1376]{1,0:T(8,128)}), f32[24,1376]{1,0:T(8,128)}) %all-reduce.8.cloned.1.call-update) | async-done | bytes 132112
  852.5 2.0 dynamic-slice_reduce_fusion
  (4 shorter events, 0.0 us)
Async XLA Ops:
  7.2 374.6 %copy-start = (bf16[128,128]{1,0:T(8,128)(2,1)S(1)}, bf16[128,128]{1,0:T(8,128)(2,1)}, u32[]{:S(2)}) copy-start(bf16[128,128]{1,0:T(8,128)(2,1)} %param.5) | copy-start | bytes 98308
  7.2 301.1 %all-reduce.6.cloned.1.call-start = ((), (), s32[]{:S(2)}) async-start(), calls=%async_computation.1 | async-start | bytes 135168
  10.2 0.6 copy-start.2
  10.8 356.0 %all-gather.5.cloned.1.call-start = ((), (), s32[]{:S(2)}) async-start(), calls=%async_computation.2 | async-start | bytes 2230272 | tf_op jit(solution)/shard_map/all_gather | solution.py:14
  309.9 244.0 %reduce-scatter.5.cloned.1.call-start = ((), (), s32[]{:S(2)}) async-start(), calls=%async_computation.4 | async-start | bytes 4460544
  381.7 1.6 copy-start.1
  402.0 450.5 %all-reduce.8.cloned.1.call-start = ((), (), s32[]{:S(2)}) async-start(), calls=%async_computation.3 | async-start | bytes 270336
Sparse Core Ops, SparseCore 0:
  11.8 296.4 all-reduce.5
  311.3 55.5 all-gather.4
  402.2 151.6 reduce-scatter.4
  557.0 295.4 all-reduce.7
where the time goes:
time: 862 us; the launch traced here: 861 us
  waiting for transfers between devices  788 us (91%)
  local copies, waits for them, and re-layouts  41.6 us (5%)
  between operations  14.5 us (2%)
  matrix products  10.1 us (1%)
    unnamed x7, waiting for transfers between devices  735 us
    all_gather x1, waiting for transfers between devices, on_device(): lax.all_gather(pooled.reshape(inter_count, 1, shard_len), 'intra', axis=1...  52.5 us
    unnamed x13, local copies, waits for them, and re-layouts  17.9 us
  transfers between devices with their start and end apart: 4, of which 4 were waited for; matrix products, arithmetic and copies ran while one was open for 2% of the time, Pallas kernels for 0%

commit v1 on v0

v1 whole, which is shorter than its diff:
```python
import jax
import jax.numpy as jnp
from jax import lax
from jax.experimental import pallas as pl
from jax.experimental.pallas import tpu as pltpu
from jax.sharding import Mesh, PartitionSpec as P

NZ, NYH, NYL, NX, NC = 12, 2, 4, 4, 2
NY = NYH * NYL
Y = ("yh", "yl")
ALL = ("z", "yh", "yl", "x", "c")
LANES = 128
ROWS = 12
GROUP = 43
OFFS = (0, 10, 21, 32)
SPAN = 24
STEPS = NZ // 2
BLOCKS = NC * NX * NY
CHUNK = 512


def pieces():
    for zl in range(2):
        for y in range(NY):
            for a in range(NX // 2):
                src = []
                for j in range(4):
                    block = ((j & 1) * NX + 2 * a + (j >> 1)) * NY + y
                    src.append(block * SPAN + ROWS * zl)
                yield 2 * GROUP * NY * zl + 2 * GROUP * y + GROUP * a, src


STEP_ROWS = 2 * 2 * GROUP * NY


def kernel(tok_ref, gw_ref, cot_ref, val_ref, tg_ref, pg_ref, w_ref, st_ref, p_ref, h_ref):
    rows, width = tok_ref.shape
    gain_rows = width // LANES
    zone = NZ * ROWS

    def assemble(zz, _):
        for s in range(BLOCKS):
            start = pl.multiple_of(s * zone + zz * SPAN, 8)
            st_ref[s * SPAN : (s + 1) * SPAN, :] = gw_ref[pl.ds(start, SPAN), :].astype(jnp.float32)
        out = w_ref.at[pl.ds(pl.multiple_of(zz * STEP_ROWS, 8), STEP_ROWS)]
        for base, src in pieces():
            for j in range(4):
                lo = 0 if j == 0 else 1
                t = src[j]
                out[base + OFFS[j] + lo : base + OFFS[j] + lo + 10, :] = st_ref[t + lo : t + lo + 10, :]
                if j < 3:
                    at = 10 if j == 0 else 11
                    out[base + OFFS[j + 1] : base + OFFS[j + 1] + 1, :] = (
                        st_ref[t + at : t + at + 1, :] + st_ref[src[j + 1] : src[j + 1] + 1, :]
                    )
        return 0

    lax.fori_loop(0, STEPS, assemble, 0)

    def fold(v):
        total = v[:, :LANES]
        for i in range(1, CHUNK // LANES):
            total = total + v[:, i * LANES : (i + 1) * LANES]
        return total

    def cols(k):
        return pl.ds(pl.multiple_of(k * CHUNK, CHUNK), CHUNK)

    def squares(k, acc):
        x = tok_ref[:, cols(k)].astype(jnp.float32)
        return acc + fold(x * x)

    steps = width // CHUNK
    zero = jnp.zeros((rows, LANES), jnp.float32)
    acc = lax.fori_loop(0, steps, squares, zero)
    inverse = lax.rsqrt(jnp.sum(acc, axis=1, keepdims=True) * (1.0 / width) + 1e-05)
    per = CHUNK // LANES
    cot = cot_ref[...]
    p_ref[gain_rows + width :, :] = jnp.zeros((8, LANES), jnp.float32)

    def main(k, carry):
        values, dots = carry
        normed = tok_ref[:, cols(k)].astype(jnp.float32) * inverse
        gain = jnp.concatenate([w_ref[pl.ds(k * per + i, 1), :] for i in range(per)], axis=1)
        at = pl.ds(pl.multiple_of(gain_rows + k * CHUNK, 8), CHUNK)
        weight = w_ref[at, :].astype(jnp.bfloat16)
        hidden = (normed * gain).astype(jnp.bfloat16)
        values = values + jnp.dot(hidden, weight, preferred_element_type=jnp.float32)
        p_ref[at, :] = lax.dot_general(
            hidden, cot, (((0,), (0,)), ((), ())), preferred_element_type=jnp.float32
        )
        hidden_grad = lax.dot_general(
            cot, weight, (((1,), (1,)), ((), ())), preferred_element_type=jnp.float32
        )
        gain_grad = jnp.sum(hidden_grad * normed, axis=0, keepdims=True)
        for i in range(per):
            p_ref[pl.ds(k * per + i, 1), :] = gain_grad[:, i * LANES : (i + 1) * LANES]
        normed_grad = hidden_grad * gain
        h_ref[:, cols(k)] = normed_grad
        return values, dots + fold(normed_grad * normed)

    values, dots = lax.fori_loop(0, steps, main, (zero, zero))
    val_ref[...] = values.astype(val_ref.dtype)
    mean = jnp.sum(dots, axis=1, keepdims=True) * (1.0 / width)

    def finish(k, _):
        normed = tok_ref[:, cols(k)].astype(jnp.float32) * inverse
        tg_ref[:, cols(k)] = (inverse * (h_ref[:, cols(k)] - normed * mean)).astype(tg_ref.dtype)
        return 0

    lax.fori_loop(0, steps, finish, 0)

    def split(zz, _):
        src_rows = p_ref.at[pl.ds(pl.multiple_of(zz * STEP_ROWS, 8), STEP_ROWS + 8)]
        for base, dst in pieces():
            for j in range(4):
                r = base + OFFS[j]
                st_ref[dst[j] : dst[j] + ROWS, :] = src_rows[r : r + ROWS, :]
        for s in range(BLOCKS):
            start = pl.multiple_of(s * zone + zz * SPAN, 8)
            pg_ref[pl.ds(start, SPAN), :] = st_ref[s * SPAN : (s + 1) * SPAN, :].astype(pg_ref.dtype)
        return 0

    lax.fori_loop(0, STEPS, split, 0)


def local_step(tokens, gathered, cotangent):
    rows, width = tokens.shape
    total = width // LANES + width
    vmem = pl.BlockSpec(memory_space=pltpu.VMEM)
    return pl.pallas_call(
        kernel,
        out_shape=(
            jax.ShapeDtypeStruct(cotangent.shape, jnp.bfloat16),
            jax.ShapeDtypeStruct(tokens.shape, jnp.bfloat16),
            jax.ShapeDtypeStruct(gathered.shape, jnp.bfloat16),
        ),
        in_specs=[vmem] * 3,
        out_specs=[vmem] * 3,
        scratch_shapes=[
            pltpu.VMEM((total, LANES), jnp.float32),
            pltpu.VMEM((BLOCKS * SPAN, LANES), jnp.float32),
            pltpu.VMEM((total + 8, LANES), jnp.float32),
            pltpu.VMEM((rows, width), jnp.float32),
        ],
        compiler_params=pltpu.CompilerParams(vmem_limit_bytes=48 * 1024 * 1024),
        name="local_step",
    )(tokens, gathered, cotangent)


def spread(piece, axis, count):
    return lax.all_to_all(
        jnp.broadcast_to(piece[None], (count,) + piece.shape), axis, 0, 0, tiled=True
    )


def collect(parts, axis, dtype):
    got = lax.all_to_all(parts.astype(dtype), axis, 0, 0, tiled=True)
    return jnp.sum(got.astype(jnp.float32), axis=0)


def phase():
    j = (lax.axis_index("x") % 2) * 2 + lax.axis_index("c")
    return (j * 96) % LANES


def on_device(tokens, flat_params, cotangent):
    shard_len = flat_params.shape[0]
    offset = phase()
    piece = lax.dynamic_update_slice(
        jnp.zeros((ROWS * LANES,), flat_params.dtype), flat_params, (offset,)
    ).reshape(ROWS, LANES)
    piece = spread(piece, "z", NZ).reshape(NZ * ROWS, LANES)
    piece = spread(piece, Y, NY).reshape(NY * NZ * ROWS, LANES)
    piece = spread(piece, "x", NX).reshape(NX * NY * NZ * ROWS, LANES)
    piece = spread(piece, "c", NC).reshape(BLOCKS * NZ * ROWS, LANES)
    values, token_grads, grads = local_step(tokens, piece, cotangent)
    grads = collect(grads.reshape(NC, -1, LANES), "c", jnp.bfloat16)
    grads = collect(grads.reshape(NX, -1, LANES), "x", jnp.bfloat16)
    grads = collect(grads.reshape(NY, -1, LANES), Y, jnp.bfloat16)
    grads = collect(grads.reshape(NZ, ROWS, LANES), "z", jnp.float32)
    owned = lax.dynamic_slice(grads.reshape(-1), (offset,), (shard_len,))
    return values, token_grads, owned


def solution(mesh):
    split = Mesh(mesh.devices.reshape(NZ, NYH, NYL, NX, NC), ALL)
    specs = (P(ALL, None), P(ALL), P(ALL, None))
    return jax.shard_map(
        on_device,
        mesh=split,
        in_specs=specs,
        out_specs=(P(ALL, None), P(ALL, None), P(ALL)),
        check_vma=False,
    )
```

time: 862 us -> 138 us (0.16)
  the two profiles are of different devices: /device:TPU:2 before, /device:TPU:8 now
where the time goes in v1:
time: 138 us; the launch traced here: 137 us
  blocking collectives  122 us (88%)
  Pallas kernels  11.1 us (8%)
  local copies, waits for them, and re-layouts  1.96 us (1%)
  other arithmetic  1.62 us (1%)
    all_to_all x4, blocking collectives, spread(): lax.all_to_all(jnp.broadcast_to(piece[None], (count,) + piece.shape), axi...  67 us
    all_to_all x4, blocking collectives, collect(): got = lax.all_to_all(parts.astype(dtype), axis, 0, 0, tiled=True)  54.8 us
    pallas_call x1, Pallas kernels, local_step(): pl.pallas_call(kernel, out_shape=(jax.ShapeDtypeStruct(cotangent.shape, j...  11.1 us

profile of v1, /device:TPU:8, one launch (start us, length us, event | category | flops | bytes accessed | tf_op | source)
XLA Modules:
  0.0 137.2 jit_solution(8849811725891854812)
XLA Ops:
  0.7 0.9 dynamic_update_slice.3
  1.6 25.8 %all_to_all.40 = bf16[12,12,128]{2,1,0:T(8,128)(2,1)S(1)} all-to-all(bf16[12,12,128]{2,1,0:T(8,128)(2,1)S(1)} %broadcast_in_dim.33), channel_id=1, replica_groups=mesh['z'=12,'yh'=2,'yl'=4,'x'=4,'c'=2] {'z'}, dimensions={0} | all-to-all | bytes 73728 | tf_op jit(solution)/shard_map/all_to_all | solution.py:152
  27.4 17.0 %all_to_all.41 = bf16[8,144,128]{2,1,0:T(8,128)(2,1)S(1)} all-to-all(bf16[8,144,128]{2,1,0:T(8,128)(2,1)S(1)} %broadcast_in_dim.35), channel_id=1, replica_groups=mesh['z'=12,'yh'=2,'yl'=4,'x'=4,'c'=2] {'yh','yl'}, dimensions={0} | all-to-all | bytes 589824 | tf_op jit(solution)/shard_map/all_to_all | solution.py:152
  44.5 0.2 broadcast_in_dim.37
  44.6 17.5 %all_to_all.42 = bf16[4,1152,128]{2,1,0:T(8,128)(2,1)S(1)} all-to-all(bf16[4,1152,128]{2,1,0:T(8,128)(2,1)S(1)} %broadcast_in_dim.37), channel_id=1, replica_groups=mesh['z'=12,'yh'=2,'yl'=4,'x'=4,'c'=2] {'x'}, dimensions={0} | all-to-all | bytes 2359296 | tf_op jit(solution)/shard_map/all_to_all | solution.py:152
  62.1 0.2 broadcast_in_dim.39
  62.3 0.0 copy-start
  62.3 0.0 copy-start.1
  62.3 6.7 %all_to_all.43 = bf16[2,4608,128]{2,1,0:T(8,128)(2,1)} all-to-all(bf16[2,4608,128]{2,1,0:T(8,128)(2,1)S(1)} %broadcast_in_dim.39), channel_id=1, replica_groups=mesh['z'=12,'yh'=2,'yl'=4,'x'=4,'c'=2] {'c'}, dimensions={0} | all-to-all | bytes 4718592 | tf_op jit(solution)/shard_map/all_to_all | solution.py:152
  68.9 0.0 copy-done
  68.9 0.0 copy-done.1
  68.9 11.1 %local_step.1 = (bf16[128,128]{1,0:T(8,128)(2,1)}, bf16[128,8192]{1,0:T(8,128)(2,1)}, bf16[9216,128]{1,0:T(8,128)(2,1)S(1)}) custom-call(bf16[128,8192]{1,0:T(8,128)(2,1)S(1)} %copy-done, bf16[9216,128]{1,0:T(8,128)(2,1)} %bitcast.9, bf16[128,128]{1,0:T(8,128)(2,1)S(1)} %copy-done.1), custom_call_target="tpu_custom_call" | custom-call | tf_op jit(solution)/shard_map/local_step/pallas_call | solution.py:131
  80.1 5.6 %all_to_all.44 = bf16[2,4608,128]{2,1,0:T(8,128)(2,1)S(1)} all-to-all(bf16[2,4608,128]{2,1,0:T(8,128)(2,1)S(1)} %bitcast.8), channel_id=1, replica_groups=mesh['z'=12,'yh'=2,'yl'=4,'x'=4,'c'=2] {'c'}, dimensions={0} | all-to-all | bytes 4718592 | tf_op jit(solution)/shard_map/all_to_all | solution.py:158
  85.7 1.3 reduce_sum.42
  86.9 19.5 %all_to_all.45 = bf16[4,1152,128]{2,1,0:T(8,128)(2,1)S(1)} all-to-all(bf16[4,1152,128]{2,1,0:T(8,128)(2,1)S(1)} %bitcast.11), channel_id=1, replica_groups=mesh['z'=12,'yh'=2,'yl'=4,'x'=4,'c'=2] {'x'}, dimensions={0} | all-to-all | bytes 2359296 | tf_op jit(solution)/shard_map/all_to_all | solution.py:158
  106.4 0.3 reduce_sum.43
  106.8 14.8 %all_to_all.46 = bf16[8,144,128]{2,1,0:T(8,128)(2,1)S(1)} all-to-all(bf16[8,144,128]{2,1,0:T(8,128)(2,1)S(1)} %bitcast.12), channel_id=1, replica_groups=mesh['z'=12,'yh'=2,'yl'=4,'x'=4,'c'=2] {'yh','yl'}, dimensions={0} | all-to-all | bytes 589824 | tf_op jit(solution)/shard_map/all_to_all | solution.py:158
  121.6 14.9 %all_to_all.47 = f32[12,12,128]{2,1,0:T(8,128)S(1)} all-to-all(f32[12,12,128]{2,1,0:T(8,128)S(1)} %reshape.28), channel_id=1, replica_groups=mesh['z'=12,'yh'=2,'yl'=4,'x'=4,'c'=2] {'z'}, dimensions={0} | all-to-all | bytes 147456 | tf_op jit(solution)/shard_map/all_to_all | solution.py:158
  136.5 0.7 dynamic_slice.3
  (7 shorter events, 0.1 us)
Async XLA Ops:
  62.3 6.7 %copy-start = (bf16[128,8192]{1,0:T(8,128)(2,1)S(1)}, bf16[128,8192]{1,0:T(8,128)(2,1)}, u32[]{:S(2)}) copy-start(bf16[128,8192]{1,0:T(8,128)(2,1)} %tok_ref.1) | copy-start | bytes 6291460
  62.3 6.7 %copy-start.1 = (bf16[128,128]{1,0:T(8,128)(2,1)S(1)}, bf16[128,128]{1,0:T(8,128)(2,1)}, u32[]{:S(2)}) copy-start(bf16[128,128]{1,0:T(8,128)(2,1)} %cot_ref.1) | copy-start | bytes 98308

commit v2 on v1

v2 whole, which is shorter than its diff:
```python
import jax
import jax.numpy as jnp
from jax import lax
from jax.experimental import pallas as pl
from jax.experimental.pallas import tpu as pltpu
from jax.sharding import Mesh, PartitionSpec as P

NZ, NYH, NYL, NX, NC = 12, 2, 4, 4, 2
NY = NYH * NYL
Y = ("yh", "yl")
ALL = ("z", "yh", "yl", "x", "c")
LANES = 128
ROWS = 12
GROUP = 43
OFFS = (0, 10, 21, 32)
SPAN = 24
STEPS = NZ // 2
BLOCKS = NC * NX * NY
CHUNK = 512


def pieces():
    for zl in range(2):
        for y in range(NY):
            for a in range(NX // 2):
                src = []
                for j in range(4):
                    block = ((j & 1) * NX + 2 * a + (j >> 1)) * NY + y
                    src.append(block * SPAN + ROWS * zl)
                yield 2 * GROUP * NY * zl + 2 * GROUP * y + GROUP * a, src


STEP_ROWS = 2 * 2 * GROUP * NY


def fold(v):
    total = v[:, :LANES]
    for i in range(1, v.shape[1] // LANES):
        total = total + v[:, i * LANES : (i + 1) * LANES]
    return total


def squares_kernel(tok_ref, out_ref):
    total = jnp.zeros(out_ref.shape, jnp.float32)
    for i in range(0, tok_ref.shape[1], CHUNK):
        x = tok_ref[:, i : i + CHUNK].astype(jnp.float32)
        total = total + fold(x * x)
    out_ref[...] = total


def finish_kernel(tok_ref, wb_ref, gain_ref, cot_ref, stat_ref, out_ref):
    inverse, mean = stat_ref[0, :, :1], stat_ref[1, :, :1]
    per = CHUNK // LANES
    for k in range(tok_ref.shape[1] // CHUNK):
        at = slice(k * CHUNK, (k + 1) * CHUNK)
        hidden_grad = lax.dot_general(
            cot_ref[...], wb_ref[at, :], (((1,), (1,)), ((), ())), preferred_element_type=jnp.float32
        )
        gain = jnp.concatenate([gain_ref[k * per + n : k * per + n + 1, :] for n in range(per)], axis=1)
        normed = tok_ref[:, at].astype(jnp.float32) * inverse
        out_ref[:, at] = (inverse * (hidden_grad * gain - normed * mean)).astype(out_ref.dtype)


def kernel(
    tok_ref, own_ref, oth_ref, cot_ref, sq_ref,
    val_ref, wb_ref, gain_ref, stat_ref, keep_ref, send_ref,
    w_ref, st_ref, p_ref,
):
    rows, width = tok_ref.shape
    gain_rows = width // LANES
    zone = NZ * ROWS
    mine = core()
    half = BLOCKS // 2 * SPAN

    def region(stage, core_at):
        return stage.at[pl.ds(pl.multiple_of(core_at * half, half), half)]

    for zz in range(STEPS):
        stage = st_ref.at[zz % 2]
        for core_at, ref in ((mine, own_ref), (1 - mine, oth_ref)):
            to = region(stage, core_at)
            for s in range(BLOCKS // 2):
                start = s * zone + zz * SPAN
                to[s * SPAN : (s + 1) * SPAN, :] = ref[start : start + SPAN, :].astype(jnp.float32)
        for base, src in pieces():
            base = base + zz * STEP_ROWS
            for j in range(4):
                lo = 0 if j == 0 else 1
                t = src[j]
                w_ref[base + OFFS[j] + lo : base + OFFS[j] + lo + 10, :] = stage[t + lo : t + lo + 10, :]
                if j < 3:
                    at = 10 if j == 0 else 11
                    w_ref[base + OFFS[j + 1] : base + OFFS[j + 1] + 1, :] = (
                        stage[t + at : t + at + 1, :] + stage[src[j + 1] : src[j + 1] + 1, :]
                    )

    def cols(k):
        return pl.ds(pl.multiple_of(k * CHUNK, CHUNK), CHUNK)

    steps = width // CHUNK
    zero = jnp.zeros((rows, LANES), jnp.float32)
    inverse = lax.rsqrt(jnp.sum(sq_ref[...], axis=1, keepdims=True) * (1.0 / width) + 1e-05)
    per = CHUNK // LANES
    cot = cot_ref[...]
    p_ref[gain_rows + width :, :] = jnp.zeros((8, LANES), jnp.float32)

    def main(k, carry):
        values, dots = carry
        normed = tok_ref[:, cols(k)].astype(jnp.float32) * inverse
        gain = jnp.concatenate([w_ref[pl.ds(k * per + i, 1), :] for i in range(per)], axis=1)
        at = pl.ds(pl.multiple_of(gain_rows + k * CHUNK, 8), CHUNK)
        weight = w_ref[at, :].astype(jnp.bfloat16)
        wb_ref[pl.ds(pl.multiple_of(k * CHUNK, CHUNK), CHUNK), :] = weight
        hidden = (normed * gain).astype(jnp.bfloat16)
        values = values + jnp.dot(hidden, weight, preferred_element_type=jnp.float32)
        p_ref[at, :] = lax.dot_general(
            hidden, cot, (((0,), (0,)), ((), ())), preferred_element_type=jnp.float32
        )
        hidden_grad = lax.dot_general(
            cot, weight, (((1,), (1,)), ((), ())), preferred_element_type=jnp.float32
        )
        gain_grad = jnp.sum(hidden_grad * normed, axis=0, keepdims=True)
        for i in range(per):
            p_ref[pl.ds(k * per + i, 1), :] = gain_grad[:, i * LANES : (i + 1) * LANES]
        return values, dots + fold(hidden_grad * gain * normed)

    values, dots = lax.fori_loop(0, steps, main, (zero, zero), unroll=True)
    val_ref[...] = values.astype(val_ref.dtype)
    mean = jnp.sum(dots, axis=1, keepdims=True) * (1.0 / width)

    gain_ref[...] = w_ref[:gain_rows, :]
    stat_ref[0, :, :] = jnp.broadcast_to(inverse, (rows, LANES))
    stat_ref[1, :, :] = jnp.broadcast_to(mean, (rows, LANES))

    for zz in range(STEPS):
        stage = st_ref.at[zz % 2]
        for base, dst in pieces():
            for j in range(4):
                r = base + zz * STEP_ROWS + OFFS[j]
                stage[dst[j] : dst[j] + ROWS, :] = p_ref[r : r + ROWS, :]
        for core_at, ref in ((mine, keep_ref), (1 - mine, send_ref)):
            of = region(stage, core_at)
            for s in range(BLOCKS // 2):
                start = s * zone + zz * SPAN
                ref[start : start + SPAN, :] = of[s * SPAN : (s + 1) * SPAN, :].astype(ref.dtype)


def core():
    return lax.axis_index("c")


def call(body, outs, scratch, mib, flops, *args):
    vmem = pl.BlockSpec(memory_space=pltpu.VMEM)
    moved = sum(a.size * a.dtype.itemsize for a in (*args, *outs))
    return pl.pallas_call(
        body,
        out_shape=outs,
        in_specs=[vmem] * len(args),
        out_specs=tuple([vmem] * len(outs)),
        scratch_shapes=scratch,
        compiler_params=pltpu.CompilerParams(vmem_limit_bytes=mib * 1024 * 1024),
        cost_estimate=pl.CostEstimate(flops=flops, bytes_accessed=moved, transcendentals=0),
    )(*args)


def squares(tokens):
    rows, _ = tokens.shape
    outs = (jax.ShapeDtypeStruct((rows, LANES), jnp.float32),)
    return call(squares_kernel, outs, [], 8, 2 * tokens.size, tokens)[0]


def finish(tokens, weight, gain, cotangent, stats):
    outs = (jax.ShapeDtypeStruct(tokens.shape, tokens.dtype),)
    flops = 2 * tokens.size * LANES
    return call(finish_kernel, outs, [], 12, flops, tokens, weight, gain, cotangent, stats)[0]


def local_step(tokens, own, other, cotangent, squared):
    rows, width = tokens.shape
    total = width // LANES + width
    outs = (
        jax.ShapeDtypeStruct(cotangent.shape, jnp.bfloat16),
        jax.ShapeDtypeStruct((width, LANES), jnp.bfloat16),
        jax.ShapeDtypeStruct((width // LANES, LANES), jnp.float32),
        jax.ShapeDtypeStruct((2, rows, LANES), jnp.float32),
        jax.ShapeDtypeStruct(own.shape, jnp.bfloat16),
        jax.ShapeDtypeStruct(own.shape, jnp.bfloat16),
    )
    scratch = [
        pltpu.VMEM((total, LANES), jnp.float32),
        pltpu.VMEM((2, BLOCKS * SPAN, LANES), jnp.float32),
        pltpu.VMEM((total + 8, LANES), jnp.float32),
    ]
    flops = 6 * tokens.size * LANES
    return call(kernel, outs, scratch, 24, flops, tokens, own, other, cotangent, squared)


def spread(piece, axis, count):
    return lax.all_to_all(
        jnp.broadcast_to(piece[None], (count,) + piece.shape), axis, 0, 0, tiled=True
    )


def collect(parts, axis, dtype):
    got = lax.all_to_all(parts.astype(dtype), axis, 0, 0, tiled=True)
    return jnp.sum(got.astype(jnp.float32), axis=0)


def swap(half):
    return lax.ppermute(half, "c", ((0, 1), (1, 0)))


def phase():
    j = (lax.axis_index("x") % 2) * 2 + lax.axis_index("c")
    return (j * 96) % LANES


def program(tokens, flat_params, cotangent):
    shard_len = flat_params.shape[0]
    offset = phase()
    piece = lax.dynamic_update_slice(
        jnp.zeros((ROWS * LANES,), flat_params.dtype), flat_params, (offset,)
    ).reshape(ROWS, LANES)
    piece = spread(piece, "z", NZ).reshape(NZ * ROWS, LANES)
    piece = spread(piece, Y, NY).reshape(NY * NZ * ROWS, LANES)
    piece = spread(piece, "x", NX).reshape(NX * NY * NZ * ROWS, LANES)
    other = swap(piece)
    values, weight, gain, stats, kept, sent = local_step(
        tokens, piece, other, cotangent, squares(tokens)
    )
    token_grads = finish(tokens, weight, gain, cotangent, stats)
    grads = kept.astype(jnp.float32) + swap(sent).astype(jnp.float32)
    grads = collect(grads.reshape(NX, -1, LANES), "x", jnp.bfloat16)
    grads = collect(grads.reshape(NY, -1, LANES), Y, jnp.bfloat16)
    grads = collect(grads.reshape(NZ, ROWS, LANES), "z", jnp.float32)
    owned = lax.dynamic_slice(grads.reshape(-1), (offset,), (shard_len,))
    return values, token_grads, owned


def solution(mesh):
    split = Mesh(mesh.devices.reshape(NZ, NYH, NYL, NX, NC), ALL)
    specs = (P(ALL, None), P(ALL), P(ALL, None))
    return jax.shard_map(
        program,
        mesh=split,
        in_specs=specs,
        out_specs=(P(ALL, None), P(ALL, None), P(ALL)),
        check_vma=False,
    )
```

time: 138 us -> 131 us (0.949)
  the two profiles are of different devices: /device:TPU:8 before, /device:TPU:2 now
where the time goes in v2:
time: 131 us
  blocking collectives  95.8 us (73%)
  waiting for transfers between devices  12.7 us (10%)
  Pallas kernels  8.58 us (7%)
  starting transfers between devices  7.58 us (6%)
  local copies, waits for them, and re-layouts  4.03 us (3%)
    all_to_all x3, blocking collectives, spread(): lax.all_to_all(jnp.broadcast_to(piece[None], (count,) + piece.shape), axi...  60.7 us
    all_to_all x2, blocking collectives, collect(): got = lax.all_to_all(parts.astype(dtype), axis, 0, 0, tiled=True)  35.1 us
    pallas_call x3, Pallas kernels, call(): pl.pallas_call(body, out_shape=outs, in_specs=[vmem] * len(args), out_spe...  8.58 us
    all_to_all x1, waiting for transfers between devices, collect(): got = lax.all_to_all(parts.astype(dtype), axis, 0, 0, tiled=True)  7.59 us
    ppermute x2, waiting for transfers between devices, swap(): return lax.ppermute(half, 'c', ((0, 1), (1, 0)))  5.07 us
    ppermute x2, starting transfers between devices, swap(): return lax.ppermute(half, 'c', ((0, 1), (1, 0)))  4.08 us
    all_to_all x1, starting transfers between devices, collect(): got = lax.all_to_all(parts.astype(dtype), axis, 0, 0, tiled=True)  3.51 us
  transfers between devices with their start and end apart: 3, of which 3 were waited for; matrix products, arithmetic and copies ran while one was open for 0% of the time, Pallas kernels for 2%

profile of v2, /device:TPU:2, one launch (start us, length us, event | category | flops | bytes accessed | tf_op | source)
XLA Modules:
  0.0 130.7 jit_solution(6713024524859011278)
XLA Ops:
  0.7 0.9 dynamic_update_slice.3
  1.6 25.8 %all_to_all.30 = bf16[12,12,128]{2,1,0:T(8,128)(2,1)S(1)} all-to-all(bf16[12,12,128]{2,1,0:T(8,128)(2,1)S(1)} %broadcast_in_dim.26), channel_id=1, replica_groups=mesh['z'=12,'yh'=2,'yl'=4,'x'=4,'c'=2] {'z'}, dimensions={0} | all-to-all | bytes 73728 | tf_op jit(solution)/shard_map/all_to_all | solution.py:199
  27.4 18.0 %all_to_all.31 = bf16[8,144,128]{2,1,0:T(8,128)(2,1)S(1)} all-to-all(bf16[8,144,128]{2,1,0:T(8,128)(2,1)S(1)} %broadcast_in_dim.28), channel_id=1, replica_groups=mesh['z'=12,'yh'=2,'yl'=4,'x'=4,'c'=2] {'yh','yl'}, dimensions={0} | all-to-all | bytes 589824 | tf_op jit(solution)/shard_map/all_to_all | solution.py:199
  45.5 0.2 broadcast_in_dim.30
  45.6 0.0 copy-start
  45.7 16.8 %all_to_all.32 = bf16[4,1152,128]{2,1,0:T(8,128)(2,1)S(1)} all-to-all(bf16[4,1152,128]{2,1,0:T(8,128)(2,1)S(1)} %broadcast_in_dim.30), channel_id=1, replica_groups=mesh['z'=12,'yh'=2,'yl'=4,'x'=4,'c'=2] {'x'}, dimensions={0} | all-to-all | bytes 2359296 | tf_op jit(solution)/shard_map/all_to_all | solution.py:199
  62.5 0.0 copy-start.3
  62.5 2.0 %collective-permute-start = (bf16[4608,128]{1,0:T(8,128)(2,1)S(1)}, bf16[4608,128]{1,0:T(8,128)(2,1)S(1)}, u32[]{:S(2)}, u32[]{:S(2)}) collective-permute-start(bf16[4608,128]{1,0:T(8,128)(2,1)S(1)} %bitcast.6), channel_id=1, source_target_pairs={{0,1},{1,0},{2,3},{3,2},{4,5},{5,4},{6,7},{7,6},{8,9},{9,8},{10,11... | collective-permute-start | bytes 3538952 | tf_op jit(solution)/shard_map/ppermute | solution.py:210
  64.5 0.0 copy-done
  64.5 0.4 shard_map.58.sq_ref
  64.9 2.4 %collective-permute-done.oth_ref = bf16[4608,128]{1,0:T(8,128)(2,1)S(1)} collective-permute-done((bf16[4608,128]{1,0:T(8,128)(2,1)S(1)}, bf16[4608,128]{1,0:T(8,128)(2,1)S(1)}, u32[]{:S(2)}, u32[]{:S(2)}) %collective-permute-start) | collective-permute-done | bytes 1179680 | tf_op jit(solution)/shard_map/ppermute | solution.py:210
  67.3 0.0 copy-done.3
  67.3 5.8 %shard_map.59 = (bf16[128,128]{1,0:T(8,128)(2,1)}, bf16[8192,128]{1,0:T(8,128)(2,1)S(1)}, f32[64,128]{1,0:T(8,128)S(1)}, f32[2,128,128]{2,1,0:T(8,128)S(1)}, bf1...) custom-call(bf16[128,8192]{1,0:T(8,128)(2,1)S(1)} %copy-done, bf16[4608,128]{1,0:T(8,128)(2,1)S(1)} %bitcast.7, ...), custom_call_target="tpu_custom_call" | custom-call | flops 805306368 | bytes 9207808 | tf_op jit(solution)/shard_map/pallas_call | solution.py:155
  73.2 0.0 copy-start.1
  73.2 2.0 %collective-permute-start.1 = (bf16[4608,128]{1,0:T(8,128)(2,1)S(1)}, bf16[4608,128]{1,0:T(8,128)(2,1)S(1)}, u32[]{:S(2)}, u32[]{:S(2)}) collective-permute-start(bf16[4608,128]{1,0:T(8,128)(2,1)S(1)} %get-tuple-element.14), channel_id=1, source_target_pairs={{0,1},{1,0},{2,3},{3,2},{4,5},{5,4},{6,7},{7,6},{8,9},{9,8},{10,11... | collective-permute-start | bytes 3538952 | tf_op jit(solution)/shard_map/ppermute | solution.py:210
  75.2 2.7 %collective-permute-done.1 = bf16[4608,128]{1,0:T(8,128)(2,1)S(1)} collective-permute-done((bf16[4608,128]{1,0:T(8,128)(2,1)S(1)}, bf16[4608,128]{1,0:T(8,128)(2,1)S(1)}, u32[]{:S(2)}, u32[]{:S(2)}) %collective-permute-start.1) | collective-permute-done | bytes 1179680 | tf_op jit(solution)/shard_map/ppermute | solution.py:210
  77.9 0.3 add_convert_fusion
  78.2 0.0 copy-done.1
  78.2 19.5 %all_to_all.33 = bf16[4,1152,128]{2,1,0:T(8,128)(2,1)S(1)} all-to-all(bf16[4,1152,128]{2,1,0:T(8,128)(2,1)S(1)} %bitcast.8), channel_id=1, replica_groups=mesh['z'=12,'yh'=2,'yl'=4,'x'=4,'c'=2] {'x'}, dimensions={0} | all-to-all | bytes 2359296 | tf_op jit(solution)/shard_map/all_to_all | solution.py:205
  97.7 0.9 reduce_sum.30
  98.7 15.6 %all_to_all.34 = bf16[8,144,128]{2,1,0:T(8,128)(2,1)S(1)} all-to-all(bf16[8,144,128]{2,1,0:T(8,128)(2,1)} %bitcast.9), channel_id=1, replica_groups=mesh['z'=12,'yh'=2,'yl'=4,'x'=4,'c'=2] {'yh','yl'}, dimensions={0} | all-to-all | bytes 589824 | tf_op jit(solution)/shard_map/all_to_all | solution.py:205
  114.3 0.6 reshape.23
  115.0 3.5 %all-to-all-start.5 = ((f32[12,12,128]{2,1,0:T(8,128)}), f32[12,12,128]{2,1,0:T(8,128)S(1)}, u32[]{:S(2)}, u32[]{:S(2)}) async-start(f32[12,12,128]{2,1,0:T(8,128)} %reshape.23), calls=%async_computation.5 | async-start | bytes 196608 | tf_op jit(solution)/shard_map/all_to_all | solution.py:205
  118.5 0.0 copy-start.2
  118.5 1.6 %copy-done.2 = bf16[8192,128]{1,0:T(8,128)(2,1)S(1)} copy-done((bf16[8192,128]{1,0:T(8,128)(2,1)S(1)}, bf16[8192,128]{1,0:T(8,128)(2,1)}, u32[]{:S(2)}) %copy-start.2) | copy-done | bytes 2097176
  120.1 2.3 %shard_map.60 = bf16[128,8192]{1,0:T(8,128)(2,1)} custom-call(bf16[128,8192]{1,0:T(8,128)(2,1)S(1)} %copy-done, bf16[8192,128]{1,0:T(8,128)(2,1)S(1)} %copy-done.2, f32[64,128]{1,0:T(8,128)S(1)} %get-tuple-element.11.gain_ref, bf16[128,128]{1,0:T(8,128)(2,1)S(1)} %copy-done.3, f32[2,128,128]{2,1,0:T(8,128)S(1)} %get-tuple-element.12.stat_ref), custom_call_target="tpu_custom_call" | custom-call | flops 268435456 | bytes 6488064 | tf_op jit(solution)/shard_map/pallas_call | solution.py:155
  122.4 7.6 %all-to-all-done.5 = f32[12,12,128]{2,1,0:T(8,128)S(1)} async-done(((f32[12,12,128]{2,1,0:T(8,128)}), f32[12,12,128]{2,1,0:T(8,128)S(1)}, u32[]{:S(2)}, u32[]{:S(2)}) %all-to-all-start.5) | async-done | bytes 73760 | tf_op jit(solution)/shard_map/all_to_all | solution.py:205
  130.0 0.7 dynamic_slice.3
  (6 shorter events, 0.1 us)
Async XLA Ops:
  45.6 18.9 %copy-start = (bf16[128,8192]{1,0:T(8,128)(2,1)S(1)}, bf16[128,8192]{1,0:T(8,128)(2,1)}, u32[]{:S(2)}) copy-start(bf16[128,8192]{1,0:T(8,128)(2,1)} %tok_ref.5) | copy-start | bytes 6291460
  62.5 4.9 %copy-start.3 = (bf16[128,128]{1,0:T(8,128)(2,1)S(1)}, bf16[128,128]{1,0:T(8,128)(2,1)}, u32[]{:S(2)}) copy-start(bf16[128,128]{1,0:T(8,128)(2,1)} %cot_ref.3) | copy-start | bytes 98308
  62.5 4.9 %collective-permute-start = (bf16[4608,128]{1,0:T(8,128)(2,1)S(1)}, bf16[4608,128]{1,0:T(8,128)(2,1)S(1)}, u32[]{:S(2)}, u32[]{:S(2)}) collective-permute-start(bf16[4608,128]{1,0:T(8,128)(2,1)S(1)} %bitcast.6), channel_id=1, source_target_pairs={{0,1},{1,0},{2,3},{3,2},{4,5},{5,4},{6,7},{7,6},{8,9},{9,8},{10,11... | collective-permute-start | bytes 3538952 | tf_op jit(solution)/shard_map/ppermute | solution.py:210
  73.2 5.0 %copy-start.1 = (bf16[8192,128]{1,0:T(8,128)(2,1)}, bf16[8192,128]{1,0:T(8,128)(2,1)S(1)}, u32[]{:S(2)}) copy-start(bf16[8192,128]{1,0:T(8,128)(2,1)S(1)} %get-tuple-element.10.wb_ref) | copy-start | bytes 6291460
  73.2 4.7 %collective-permute-start.1 = (bf16[4608,128]{1,0:T(8,128)(2,1)S(1)}, bf16[4608,128]{1,0:T(8,128)(2,1)S(1)}, u32[]{:S(2)}, u32[]{:S(2)}) collective-permute-start(bf16[4608,128]{1,0:T(8,128)(2,1)S(1)} %get-tuple-element.14), channel_id=1, source_target_pairs={{0,1},{1,0},{2,3},{3,2},{4,5},{5,4},{6,7},{7,6},{8,9},{9,8},{10,11... | collective-permute-start | bytes 3538952 | tf_op jit(solution)/shard_map/ppermute | solution.py:210
  115.0 15.0 %all-to-all-start.5 = ((f32[12,12,128]{2,1,0:T(8,128)}), f32[12,12,128]{2,1,0:T(8,128)S(1)}, u32[]{:S(2)}, u32[]{:S(2)}) async-start(f32[12,12,128]{2,1,0:T(8,128)} %reshape.23), calls=%async_computation.5 | async-start | bytes 196608 | tf_op jit(solution)/shard_map/all_to_all | solution.py:205
  118.5 1.6 %copy-start.2 = (bf16[8192,128]{1,0:T(8,128)(2,1)S(1)}, bf16[8192,128]{1,0:T(8,128)(2,1)}, u32[]{:S(2)}) copy-start(bf16[8192,128]{1,0:T(8,128)(2,1)} %copy-done.1) | copy-start | bytes 6291460

commit v3 on v2

--- a/solution.py
+++ b/solution.py
@@ -64,7 +64,7 @@
 def kernel(
     tok_ref, own_ref, oth_ref, cot_ref, sq_ref,
     val_ref, wb_ref, gain_ref, stat_ref, keep_ref, send_ref,
-    w_ref, st_ref, p_ref,
+    w_ref, st0_ref, st1_ref, p_ref,
 ):
     rows, width = tok_ref.shape
     gain_rows = width // LANES
@@ -76,7 +76,7 @@
         return stage.at[pl.ds(pl.multiple_of(core_at * half, half), half)]
 
     for zz in range(STEPS):
-        stage = st_ref.at[zz % 2]
+        stage = (st0_ref, st1_ref)[zz % 2]
         for core_at, ref in ((mine, own_ref), (1 - mine, oth_ref)):
             to = region(stage, core_at)
             for s in range(BLOCKS // 2):
@@ -133,7 +133,7 @@
     stat_ref[1, :, :] = jnp.broadcast_to(mean, (rows, LANES))
 
     for zz in range(STEPS):
-        stage = st_ref.at[zz % 2]
+        stage = (st0_ref, st1_ref)[zz % 2]
         for base, dst in pieces():
             for j in range(4):
                 r = base + zz * STEP_ROWS + OFFS[j]
@@ -188,7 +188,8 @@
     )
     scratch = [
         pltpu.VMEM((total, LANES), jnp.float32),
-        pltpu.VMEM((2, BLOCKS * SPAN, LANES), jnp.float32),
+        pltpu.VMEM((BLOCKS * SPAN, LANES), jnp.float32),
+        pltpu.VMEM((BLOCKS * SPAN, LANES), jnp.float32),
         pltpu.VMEM((total + 8, LANES), jnp.float32),
     ]
     flops = 6 * tokens.size * LANES
@@ -232,7 +233,7 @@
     grads = kept.astype(jnp.float32) + swap(sent).astype(jnp.float32)
     grads = collect(grads.reshape(NX, -1, LANES), "x", jnp.bfloat16)
     grads = collect(grads.reshape(NY, -1, LANES), Y, jnp.bfloat16)
-    grads = collect(grads.reshape(NZ, ROWS, LANES), "z", jnp.float32)
+    grads = collect(grads.reshape(NZ, ROWS, LANES), "z", jnp.bfloat16)
     owned = lax.dynamic_slice(grads.reshape(-1), (offset,), (shard_len,))
     return values, token_grads, owned
 

time: 131 us -> 130 us (level)
  no operation moved by 1% of the time
where the time goes in v3:
time: 130 us
  blocking collectives  95.9 us (74%)
  waiting for transfers between devices  11.8 us (9%)
  Pallas kernels  8.3 us (6%)
  starting transfers between devices  7.59 us (6%)
  local copies, waits for them, and re-layouts  4.02 us (3%)
  other arithmetic  1.3 us (1%)
    all_to_all x3, blocking collectives, spread(): lax.all_to_all(jnp.broadcast_to(piece[None], (count,) + piece.shape), axi...  60.7 us
    all_to_all x2, blocking collectives, collect(): got = lax.all_to_all(parts.astype(dtype), axis, 0, 0, tiled=True)  35.2 us
    pallas_call x3, Pallas kernels, call(): pl.pallas_call(body, out_shape=outs, in_specs=[vmem] * len(args), out_spe...  8.3 us
    all_to_all x1, waiting for transfers between devices, collect(): got = lax.all_to_all(parts.astype(dtype), axis, 0, 0, tiled=True)  6.8 us
    ppermute x2, waiting for transfers between devices, swap(): return lax.ppermute(half, 'c', ((0, 1), (1, 0)))  5.04 us
    ppermute x2, starting transfers between devices, swap(): return lax.ppermute(half, 'c', ((0, 1), (1, 0)))  4.11 us
    all_to_all x1, starting transfers between devices, collect(): got = lax.all_to_all(parts.astype(dtype), axis, 0, 0, tiled=True)  3.48 us
  transfers between devices with their start and end apart: 3, of which 3 were waited for; matrix products, arithmetic and copies ran while one was open for 0% of the time, Pallas kernels for 2%

profile of v3, /device:TPU:2, one launch (start us, length us, event | category | flops | bytes accessed | tf_op | source)
XLA Modules:
  0.0 129.7 jit_solution(1975868935439433460)
XLA Ops:
  0.7 0.9 dynamic_update_slice.3
  1.6 25.8 %all_to_all.30 = bf16[12,12,128]{2,1,0:T(8,128)(2,1)S(1)} all-to-all(bf16[12,12,128]{2,1,0:T(8,128)(2,1)S(1)} %broadcast_in_dim.26), channel_id=1, replica_groups=mesh['z'=12,'yh'=2,'yl'=4,'x'=4,'c'=2] {'z'}, dimensions={0} | all-to-all | bytes 73728 | tf_op jit(solution)/shard_map/all_to_all | solution.py:200
  27.4 18.0 %all_to_all.31 = bf16[8,144,128]{2,1,0:T(8,128)(2,1)S(1)} all-to-all(bf16[8,144,128]{2,1,0:T(8,128)(2,1)S(1)} %broadcast_in_dim.28), channel_id=1, replica_groups=mesh['z'=12,'yh'=2,'yl'=4,'x'=4,'c'=2] {'yh','yl'}, dimensions={0} | all-to-all | bytes 589824 | tf_op jit(solution)/shard_map/all_to_all | solution.py:200
  45.5 0.2 broadcast_in_dim.30
  45.6 0.0 copy-start
  45.7 16.8 %all_to_all.32 = bf16[4,1152,128]{2,1,0:T(8,128)(2,1)S(1)} all-to-all(bf16[4,1152,128]{2,1,0:T(8,128)(2,1)S(1)} %broadcast_in_dim.30), channel_id=1, replica_groups=mesh['z'=12,'yh'=2,'yl'=4,'x'=4,'c'=2] {'x'}, dimensions={0} | all-to-all | bytes 2359296 | tf_op jit(solution)/shard_map/all_to_all | solution.py:200
  62.5 0.0 copy-start.3
  62.5 2.0 %collective-permute-start = (bf16[4608,128]{1,0:T(8,128)(2,1)S(1)}, bf16[4608,128]{1,0:T(8,128)(2,1)S(1)}, u32[]{:S(2)}, u32[]{:S(2)}) collective-permute-start(bf16[4608,128]{1,0:T(8,128)(2,1)S(1)} %bitcast.6), channel_id=1, source_target_pairs={{0,1},{1,0},{2,3},{3,2},{4,5},{5,4},{6,7},{7,6},{8,9},{9,8},{10,11... | collective-permute-start | bytes 3538952 | tf_op jit(solution)/shard_map/ppermute | solution.py:211
  64.5 0.0 copy-done
  64.5 0.4 shard_map.58.sq_ref
  64.9 2.4 %collective-permute-done.oth_ref = bf16[4608,128]{1,0:T(8,128)(2,1)S(1)} collective-permute-done((bf16[4608,128]{1,0:T(8,128)(2,1)S(1)}, bf16[4608,128]{1,0:T(8,128)(2,1)S(1)}, u32[]{:S(2)}, u32[]{:S(2)}) %collective-permute-start) | collective-permute-done | bytes 1179680 | tf_op jit(solution)/shard_map/ppermute | solution.py:211
  67.3 0.0 copy-done.3
  67.3 5.5 %shard_map.59 = (bf16[128,128]{1,0:T(8,128)(2,1)}, bf16[8192,128]{1,0:T(8,128)(2,1)S(1)}, f32[64,128]{1,0:T(8,128)S(1)}, f32[2,128,128]{2,1,0:T(8,128)S(1)}, bf1...) custom-call(bf16[128,8192]{1,0:T(8,128)(2,1)S(1)} %copy-done, bf16[4608,128]{1,0:T(8,128)(2,1)S(1)} %bitcast.7, ...), custom_call_target="tpu_custom_call" | custom-call | flops 805306368 | bytes 9207808 | tf_op jit(solution)/shard_map/pallas_call | solution.py:155
  72.9 0.0 copy-start.1
  72.9 2.1 %collective-permute-start.1 = (bf16[4608,128]{1,0:T(8,128)(2,1)S(1)}, bf16[4608,128]{1,0:T(8,128)(2,1)S(1)}, u32[]{:S(2)}, u32[]{:S(2)}) collective-permute-start(bf16[4608,128]{1,0:T(8,128)(2,1)S(1)} %get-tuple-element.14), channel_id=1, source_target_pairs={{0,1},{1,0},{2,3},{3,2},{4,5},{5,4},{6,7},{7,6},{8,9},{9,8},{10,11... | collective-permute-start | bytes 3538952 | tf_op jit(solution)/shard_map/ppermute | solution.py:211
  75.0 2.7 %collective-permute-done.1 = bf16[4608,128]{1,0:T(8,128)(2,1)S(1)} collective-permute-done((bf16[4608,128]{1,0:T(8,128)(2,1)S(1)}, bf16[4608,128]{1,0:T(8,128)(2,1)S(1)}, u32[]{:S(2)}, u32[]{:S(2)}) %collective-permute-start.1) | collective-permute-done | bytes 1179680 | tf_op jit(solution)/shard_map/ppermute | solution.py:211
  77.6 0.3 add_convert_fusion
  77.9 0.0 copy-done.1
  77.9 19.5 %all_to_all.33 = bf16[4,1152,128]{2,1,0:T(8,128)(2,1)S(1)} all-to-all(bf16[4,1152,128]{2,1,0:T(8,128)(2,1)S(1)} %bitcast.8), channel_id=1, replica_groups=mesh['z'=12,'yh'=2,'yl'=4,'x'=4,'c'=2] {'x'}, dimensions={0} | all-to-all | bytes 2359296 | tf_op jit(solution)/shard_map/all_to_all | solution.py:206
  97.5 0.9 reduce_sum.33
  98.4 15.7 %all_to_all.34 = bf16[8,144,128]{2,1,0:T(8,128)(2,1)S(1)} all-to-all(bf16[8,144,128]{2,1,0:T(8,128)(2,1)} %bitcast.10), channel_id=1, replica_groups=mesh['z'=12,'yh'=2,'yl'=4,'x'=4,'c'=2] {'yh','yl'}, dimensions={0} | all-to-all | bytes 589824 | tf_op jit(solution)/shard_map/all_to_all | solution.py:206
  114.1 0.6 convert_element_type.30
  114.7 3.5 %all-to-all-start.5 = ((bf16[12,12,128]{2,1,0:T(8,128)(2,1)}), bf16[12,12,128]{2,1,0:T(8,128)(2,1)S(1)}, u32[]{:S(2)}, u32[]{:S(2)}) async-start(bf16[12,12,128]{2,1,0:T(8,128)(2,1)} %convert_element_type.30), calls=%async_computation.5 | async-start | bytes 98304 | tf_op jit(solution)/shard_map/all_to_all | solution.py:206
  118.2 0.0 copy-start.2
  118.2 1.6 %copy-done.2 = bf16[8192,128]{1,0:T(8,128)(2,1)S(1)} copy-done((bf16[8192,128]{1,0:T(8,128)(2,1)S(1)}, bf16[8192,128]{1,0:T(8,128)(2,1)}, u32[]{:S(2)}) %copy-start.2) | copy-done | bytes 2097176
  119.8 2.3 %shard_map.60 = bf16[128,8192]{1,0:T(8,128)(2,1)} custom-call(bf16[128,8192]{1,0:T(8,128)(2,1)S(1)} %copy-done, bf16[8192,128]{1,0:T(8,128)(2,1)S(1)} %copy-done.2, f32[64,128]{1,0:T(8,128)S(1)} %get-tuple-element.11.gain_ref, bf16[128,128]{1,0:T(8,128)(2,1)S(1)} %copy-done.3, f32[2,128,128]{2,1,0:T(8,128)S(1)} %get-tuple-element.12.stat_ref), custom_call_target="tpu_custom_call" | custom-call | flops 268435456 | bytes 6488064 | tf_op jit(solution)/shard_map/pallas_call | solution.py:155
  122.2 6.8 %all-to-all-done.5 = bf16[12,12,128]{2,1,0:T(8,128)(2,1)S(1)} async-done(((bf16[12,12,128]{2,1,0:T(8,128)(2,1)}), bf16[12,12,128]{2,1,0:T(8,128)(2,1)S(1)}, u32[]{:S(2)}, u32[]{:S(2)}) %all-to-all-start.5) | async-done | bytes 36896 | tf_op jit(solution)/shard_map/all_to_all | solution.py:206
  129.0 0.7 dynamic_slice.3
  (6 shorter events, 0.1 us)
Async XLA Ops:
  45.6 18.9 %copy-start = (bf16[128,8192]{1,0:T(8,128)(2,1)S(1)}, bf16[128,8192]{1,0:T(8,128)(2,1)}, u32[]{:S(2)}) copy-start(bf16[128,8192]{1,0:T(8,128)(2,1)} %tok_ref.5) | copy-start | bytes 6291460
  62.5 4.9 %copy-start.3 = (bf16[128,128]{1,0:T(8,128)(2,1)S(1)}, bf16[128,128]{1,0:T(8,128)(2,1)}, u32[]{:S(2)}) copy-start(bf16[128,128]{1,0:T(8,128)(2,1)} %cot_ref.3) | copy-start | bytes 98308
  62.5 4.9 %collective-permute-start = (bf16[4608,128]{1,0:T(8,128)(2,1)S(1)}, bf16[4608,128]{1,0:T(8,128)(2,1)S(1)}, u32[]{:S(2)}, u32[]{:S(2)}) collective-permute-start(bf16[4608,128]{1,0:T(8,128)(2,1)S(1)} %bitcast.6), channel_id=1, source_target_pairs={{0,1},{1,0},{2,3},{3,2},{4,5},{5,4},{6,7},{7,6},{8,9},{9,8},{10,11... | collective-permute-start | bytes 3538952 | tf_op jit(solution)/shard_map/ppermute | solution.py:211
  72.9 5.0 %copy-start.1 = (bf16[8192,128]{1,0:T(8,128)(2,1)}, bf16[8192,128]{1,0:T(8,128)(2,1)S(1)}, u32[]{:S(2)}) copy-start(bf16[8192,128]{1,0:T(8,128)(2,1)S(1)} %get-tuple-element.10.wb_ref) | copy-start | bytes 6291460
  72.9 4.7 %collective-permute-start.1 = (bf16[4608,128]{1,0:T(8,128)(2,1)S(1)}, bf16[4608,128]{1,0:T(8,128)(2,1)S(1)}, u32[]{:S(2)}, u32[]{:S(2)}) collective-permute-start(bf16[4608,128]{1,0:T(8,128)(2,1)S(1)} %get-tuple-element.14), channel_id=1, source_target_pairs={{0,1},{1,0},{2,3},{3,2},{4,5},{5,4},{6,7},{7,6},{8,9},{9,8},{10,11... | collective-permute-start | bytes 3538952 | tf_op jit(solution)/shard_map/ppermute | solution.py:211
  114.7 14.2 %all-to-all-start.5 = ((bf16[12,12,128]{2,1,0:T(8,128)(2,1)}), bf16[12,12,128]{2,1,0:T(8,128)(2,1)S(1)}, u32[]{:S(2)}, u32[]{:S(2)}) async-start(bf16[12,12,128]{2,1,0:T(8,128)(2,1)} %convert_element_type.30), calls=%async_computation.5 | async-start | bytes 98304 | tf_op jit(solution)/shard_map/all_to_all | solution.py:206
  118.2 1.6 %copy-start.2 = (bf16[8192,128]{1,0:T(8,128)(2,1)S(1)}, bf16[8192,128]{1,0:T(8,128)(2,1)}, u32[]{:S(2)}) copy-start(bf16[8192,128]{1,0:T(8,128)(2,1)} %copy-done.1) | copy-start | bytes 6291460
